TPU v7x, 512 devices: a whole 4x8x8 slice. The times are simulated.
512 devices in a mesh: rep: 64 (over x, z_hi, y), ctx: 8 (over z_lo, core).
Axes of the slice: x: 4, y: 8, z: 8 (z_hi: 2, z_lo: 4; z = z_hi * 4 + z_lo), core: 2. Of those that a mesh axis runs over, the one named last changes fastest.
Arguments:
- activations: bfloat16 [64, 1024, 4096], P('rep', 'ctx'), may hold values from -6 to 6
- queries: bfloat16 [64, 1024, 2048], P('rep', 'ctx'), may hold values from -110 to 110
- key_states: bfloat16 [64, 1024, 512], P('rep', 'ctx'), may hold values from -4 to 4
- targets: bfloat16 [64, 1024, 2048], P('rep', 'ctx'), may hold values from -1.5 to 1.5
- value_weight: bfloat16 [64, 4096, 512], P('rep', 'ctx'), may hold values from -5 to 5
- tracker: bfloat16 [64, 4096, 512], P('rep', 'ctx'), may hold values from -5 to 5
- old_gradient: bfloat16 [64, 4096, 512], P('rep', 'ctx'), may hold values from -5 to 5
Outputs:
- new_weight: bfloat16 [64, 4096, 512], P('rep', 'ctx')
- new_tracker: bfloat16 [64, 4096, 512], P('rep', 'ctx')
All inputs are finite; a program needn't handle non-finite values.
Results may differ from a plain program's by a relative error of at most 0.0095.
Values may be sent and summed in bfloat16 or wider, within the bound.
A program may use at most 64 MiB of HBM per device.

v0:
```python
import jax
import jax.numpy as jnp
from jax import lax
from jax.sharding import PartitionSpec as P

HEADS = 16
KV_HEADS = 4
HEAD_DIM = 128
ROUND = 3
step_size = 0.25
loss_weight = 16.0


def partner(shard, axis, apart):
    return lax.ppermute(shard, axis, [(i, i ^ 1 << apart) for i in range(lax.axis_size(axis))])


def local(activations, queries, key_states, targets, value_weight, tracker, old_gradient):
    token_block = activations[0]
    tokens_here = token_block.shape[0]
    value_scale = token_block.shape[1] ** (-0.5)
    grouping = HEADS // KV_HEADS
    own_weight = value_weight[0]
    weight_full = own_weight.astype(jnp.float32)
    track_full = tracker[0].astype(jnp.float32)
    old_full = old_gradient[0].astype(jnp.float32)
    feature_cols = lax.all_to_all(token_block, "ctx", split_axis=1, concat_axis=0, tiled=True)
    local_values = (
        jnp.dot(
            token_block,
            lax.all_gather(own_weight, "ctx", axis=0, tiled=True),
            preferred_element_type=jnp.float32,
        )
        * value_scale
    ).astype(jnp.bfloat16)
    all_keys, all_values = (
        lax.all_gather(key_states[0], "ctx", axis=0, tiled=True),
        lax.all_gather(local_values, "ctx", axis=0, tiled=True),
    )
    seq_total = all_keys.shape[0]
    query_heads = queries[0].reshape(tokens_here, KV_HEADS, grouping, HEAD_DIM)
    key_heads = all_keys.reshape(seq_total, KV_HEADS, HEAD_DIM)
    value_heads = all_values.reshape(seq_total, KV_HEADS, HEAD_DIM)
    scores = jnp.einsum(
        "ikgd,jkd->kgij", query_heads, key_heads, preferred_element_type=jnp.float32
    ) * HEAD_DIM ** (-0.5)
    query_pos = lax.axis_index("ctx") * tokens_here + jnp.arange(tokens_here)
    key_pos = jnp.arange(seq_total)
    allowed = key_pos[None, :] <= query_pos[:, None]
    scores = jnp.where(allowed, scores, -jnp.inf)
    highest = jnp.max(scores, axis=-1, keepdims=True)
    raised = jnp.exp(scores - highest)
    probabilities = (raised / jnp.sum(raised, axis=-1, keepdims=True)).astype(jnp.bfloat16)
    attended = jnp.einsum(
        "kgij,jkd->ikgd", probabilities, value_heads, preferred_element_type=jnp.float32
    )
    attended = attended.reshape(tokens_here, HEADS * HEAD_DIM)
    out_cot = (loss_weight * (attended - targets[0].astype(jnp.float32))).astype(jnp.bfloat16)
    cot_heads = out_cot.reshape(tokens_here, KV_HEADS, grouping, HEAD_DIM)
    value_terms = jnp.einsum(
        "kgij,ikgd->jkd", probabilities, cot_heads, preferred_element_type=jnp.float32
    )
    value_terms = value_terms.reshape(seq_total, KV_HEADS * HEAD_DIM)
    value_cot16 = lax.psum(value_terms, "ctx").astype(jnp.bfloat16)
    gradient = (
        jnp.einsum("tc,tv->cv", feature_cols, value_cot16, preferred_element_type=jnp.float32)
        * value_scale
    )
    track_half = track_full + gradient - old_full
    moved = weight_full - step_size * track_half
    peer_both = partner(jnp.stack((moved, track_half)), "rep", ROUND)
    new_weight = ((moved + peer_both[0]) * 0.5).astype(jnp.bfloat16)
    new_tracker = ((track_half + peer_both[1]) * 0.5).astype(jnp.bfloat16)
    return (new_weight[None], new_tracker[None])


def solution(mesh):
    return jax.shard_map(
        local,
        mesh=mesh,
        in_specs=(
            P("rep", "ctx", None),
            P("rep", "ctx", None),
            P("rep", "ctx", None),
            P("rep", "ctx", None),
            P("rep", "ctx", None),
            P("rep", "ctx", None),
            P("rep", "ctx", None),
        ),
        out_specs=(P("rep", "ctx", None), P("rep", "ctx", None)),
        check_vma=False,
    )
```

profile of v0, /device:TPU:1, one launch (start us, length us, event | category | flops | bytes accessed | tf_op | source)
XLA Modules:
  0.0 347.0 jit_solution(10551125804644642913)
XLA Ops:
  7.2 0.0 copy-start
  7.2 0.0 copy-start.2
  7.2 0.0 copy-start.1
  7.2 0.0 all-gather.8.cloned.1.call-start
  7.2 0.7 all-gather.8.cloned.1.call-update
  7.9 0.0 all-gather.10.cloned.1.call-start
  8.0 1.7 copy.29
  9.7 0.0 all-gather.10.cloned.1.call-update
  9.7 2.3 copy.36
  11.9 10.3 %all-to-all-start = ((bf16[128,8,512]{0,2,1:T(8,128)(2,1)}), bf16[128,8,512]{0,2,1:T(8,128)(2,1)S(1)}, u32[]{:S(2)}, u32[]{:S(2)}) async-start(bf16[128,8,512]{0,2,1:T(8,128)(2,1)} %bitcast.16), calls=%async_computation | async-start | bytes 2097152 | tf_op jit(solution)/shard_map/all_to_all | solution.py:27
  22.2 0.0 all-gather.6.cloned.1.call-start
  22.2 64.3 %all-gather.8.cloned.1.call-done = bf16[1,4096,512]{2,1,0:T(8,128)(2,1)} async-done(((bf16[1,512,512]{2,1,0:T(8,128)(2,1)}), bf16[1,4096,512]{2,1,0:T(8,128)(2,1)}) %all-gather.8.cloned.1.call-update) | async-done | bytes 4194320 | tf_op jit(solution)/shard_map/all_gather | solution.py:31
  86.6 3.9 %fusion.19 = bf16[128,512]{1,0:T(8,128)(2,1)} fusion(bf16[1,4096,512]{2,1,0:T(8,128)(2,1)} %all-gather.8.cloned.1.call-done, bf16[1,128,4096]{2,1,0:T(8,128)(2,1)} %param.7), kind=kOutput, calls=%fused_computation.22 | convolution fusion | flops 537001984 | bytes 5373952 | tf_op jit(solution)/shard_map/dot_general | solution.py:29
  90.4 0.0 all-gather.6.cloned.1.call-update
  90.5 0.0 copy-done
  90.5 0.2 copy.27
  90.7 0.0 copy-done.2
  90.7 1.2 reshape_squeeze.3
  91.9 0.0 copy-done.1
  91.9 1.2 copy.34
  93.1 1.3 copy.28
  94.3 2.0 copy.38
  96.4 0.1 iota_compare_fusion
  96.5 0.0 all-to-all-done
  96.5 1.4 copy.37
  97.8 27.6 %all-gather.10.cloned.1.call-done = bf16[1,1024,512]{1,2,0:T(8,128)(2,1)} async-done(((bf16[1,128,512]{1,2,0:T(8,128)(2,1)}), bf16[1,1024,512]{1,2,0:T(8,128)(2,1)}) %all-gather.10.cloned.1.call-update) | async-done | bytes 1048592 | tf_op jit(solution)/shard_map/all_gather | solution.py:37
  125.4 7.3 %fusion.44 = (f32[4,4,128]{2,1,0:T(4,128)S(1)}, f32[4,4,128,1024]{2,3,1,0:T(8,128)}) fusion(pred[128,1024]{0,1:T(8,128)(4,1)S(1)} %iota_compare_fusion, bf16[1024,4,128,1]{0,2,3,1:T(8,128)(2,1)} %bitcast.105, bf16[128,4,4,128]{3,2,1,0:T(4,128)(2,1)} %reshape_squeeze.3), kind=kOutput, calls=%fused_computation.46 | convolution fusion | flops 545260544 | bytes 10100736 | tf_op jit(solution)/shard_map/sub | solution.py:52
  132.7 31.0 %all-gather.6.cloned.1.call-done = bf16[1024,512]{1,0:T(8,128)(2,1)} async-done(((bf16[128,512]{1,0:T(8,128)(2,1)}), bf16[1024,512]{1,0:T(8,128)(2,1)}) %all-gather.6.cloned.1.call-update) | async-done | bytes 1048592 | tf_op jit(solution)/shard_map/all_gather | solution.py:38
  163.6 2.3 copy.46
  165.9 8.5 %fusion.15 = f32[4,128,1024,1]{2,1,3,0:T(8,128)S(1)} fusion(f32[128,4,4,128]{0,3,2,1:T(8,128)} %bitcast.102, bf16[1024,4,128,1]{0,2,3,1:T(8,128)(2,1)} %bitcast.104, f32[4,4,128,1024]{2,3,1,0:T(8,128)} %get-tuple-element.11, f32[4,4,128]{2,1,0:T(4,128)S(1)} %get-tuple-element.10), kind=kOutput, calls=%fused_computation.20 | convolution fusion | flops 1082916864 | bytes 12591104 | tf_op jit(solution)/shard_map/kgij,ikgd->jkd/dot_general | solution.py:60
  174.4 62.7 %all-reduce.1 = bf16[1024,512]{0,1:T(8,128)(2,1)} all-reduce(f32[1024,512]{0,1:T(8,128)S(1)} %bitcast.101), channel_id=1, replica_groups=mesh['rep'=64,'ctx'=8] {'ctx'}, use_global_device_ids=true, to_apply=%region_2.3 | all-reduce | flops 524288 | bytes 3145728 | tf_op jit(solution)/shard_map/psum | solution.py:64
  237.1 2.4 fusion.13
  239.5 0.2 fusion.30
  239.7 0.2 pad_maximum_fusion
  239.9 6.0 %collective-permute-start = (f32[2,512,512]{1,2,0:T(8,128)S(1)}, f32[2,512,512]{1,2,0:T(8,128)S(1)}, u32[]{:S(2)}, u32[]{:S(2)}) collective-permute-start(f32[2,512,512]{1,2,0:T(8,128)S(1)} %pad_maximum_fusion), channel_id=1, source_target_pairs={{0,64},{8,72},{16,80},{24,88},{32,96},{40,104},{48,112},{56,120},{... | collective-permute-start | bytes 6291464 | tf_op jit(solution)/shard_map/ppermute | solution.py:15
  245.9 92.1 %collective-permute-done = f32[2,512,512]{1,2,0:T(8,128)S(1)} collective-permute-done((f32[2,512,512]{1,2,0:T(8,128)S(1)}, f32[2,512,512]{1,2,0:T(8,128)S(1)}, u32[]{:S(2)}, u32[]{:S(2)}) %collective-permute-start) | collective-permute-done | bytes 2097184 | tf_op jit(solution)/shard_map/ppermute | solution.py:15
  338.0 0.5 fusion.32
  338.5 1.0 copy.39
  339.5 1.0 copy.40
  (1 shorter events, 0.0 us)
Async XLA Ops:
  7.2 83.3 %copy-start = (bf16[1,512,512]{2,1,0:T(8,128)(2,1)S(1)}, bf16[1,512,512]{2,1,0:T(8,128)(2,1)}, u32[]{:S(2)}) copy-start(bf16[1,512,512]{2,1,0:T(8,128)(2,1)} %param.11) | copy-start | bytes 1572868
  7.2 83.5 %copy-start.2 = (bf16[1,128,2048]{2,1,0:T(8,128)(2,1)S(1)}, bf16[1,128,2048]{2,1,0:T(8,128)(2,1)}, u32[]{:S(2)}) copy-start(bf16[1,128,2048]{2,1,0:T(8,128)(2,1)} %param.8) | copy-start | bytes 1572868
  7.2 84.7 %copy-start.1 = (bf16[1,128,2048]{2,1,0:T(8,128)(2,1)S(1)}, bf16[1,128,2048]{2,1,0:T(8,128)(2,1)}, u32[]{:S(2)}) copy-start(bf16[1,128,2048]{2,1,0:T(8,128)(2,1)} %param.10) | copy-start | bytes 1572868
  7.2 79.4 %all-gather.8.cloned.1.call-start = ((), (), s32[]{:S(2)}) async-start(), calls=%async_computation.2 | async-start | bytes 4718592 | tf_op jit(solution)/shard_map/all_gather | solution.py:31
  7.9 117.5 %all-gather.10.cloned.1.call-start = ((), (), s32[]{:S(2)}) async-start(), calls=%async_computation.3 | async-start | bytes 1179648 | tf_op jit(solution)/shard_map/all_gather | solution.py:37
  11.9 84.5 %all-to-all-start = ((bf16[128,8,512]{0,2,1:T(8,128)(2,1)}), bf16[128,8,512]{0,2,1:T(8,128)(2,1)S(1)}, u32[]{:S(2)}, u32[]{:S(2)}) async-start(bf16[128,8,512]{0,2,1:T(8,128)(2,1)} %bitcast.16), calls=%async_computation | async-start | bytes 2097152 | tf_op jit(solution)/shard_map/all_to_all | solution.py:27
  22.2 141.4 %all-gather.6.cloned.1.call-start = ((), (), s32[]{:S(2)}) async-start(), calls=%async_computation.1 | async-start | bytes 1179648 | tf_op jit(solution)/shard_map/all_gather | solution.py:38
  239.9 98.1 %collective-permute-start = (f32[2,512,512]{1,2,0:T(8,128)S(1)}, f32[2,512,512]{1,2,0:T(8,128)S(1)}, u32[]{:S(2)}, u32[]{:S(2)}) collective-permute-start(f32[2,512,512]{1,2,0:T(8,128)S(1)} %pad_maximum_fusion), channel_id=1, source_target_pairs={{0,64},{8,72},{16,80},{24,88},{32,96},{40,104},{48,112},{56,120},{... | collective-permute-start | bytes 6291464 | tf_op jit(solution)/shard_map/ppermute | solution.py:15
Sparse Core Ops, SparseCore 0:
  10.1 76.4 all-gather.7
  88.6 36.7 all-gather.9
  127.5 36.1 all-gather.5
where the time goes:
time: 347 us
  waiting for transfers between devices  216 us (62%)
  blocking collectives  62.7 us (18%)
  matrix products  22 us (6%)
  starting transfers between devices  16.4 us (5%)
  local copies, waits for them, and re-layouts  15.5 us (4%)
  between operations  13.8 us (4%)
    ppermute x1, waiting for transfers between devices, partner(): lax.ppermute(shard, axis, [(i, i ^ 1 << apart) for i in range(lax.axis_si...  92.1 us
    all_gather x1, waiting for transfers between devices, local(): lax.all_gather(own_weight, 'ctx', axis=0, tiled=True)  64.3 us
    psum x1, blocking collectives, local(): value_cot16 = lax.psum(value_terms, 'ctx').astype(jnp.bfloat16)  62.7 us
    all_gather x1, waiting for transfers between devices, local(): lax.all_gather(local_values, 'ctx', axis=0, tiled=True)  31 us
    all_gather x1, waiting for transfers between devices, local(): lax.all_gather(key_states[0], 'ctx', axis=0, tiled=True)  27.6 us
    all_to_all x1, starting transfers between devices, local(): lax.all_to_all(token_block, 'ctx', split_axis=1, concat_axis=0, tiled=True)  10.3 us
    unnamed x13, local copies, waits for them, and re-layouts  9.48 us
    dot_general x1, matrix products, local(): jnp.einsum('kgij,ikgd->jkd', probabilities, cot_heads, preferred_element_...  8.46 us
  transfers between devices with their start and end apart: 5, of which 4 were waited for; matrix products, arithmetic and copies ran while one was open for 6% of the time, Pallas kernels for 0%

commit v1 on v0

--- a/solution.py
+++ b/solution.py
@@ -9,6 +9,13 @@
 ROUND = 3
 step_size = 0.25
 loss_weight = 16.0
+
+
+def all_by_exchange(x, name, along):
+    peers = lax.axis_size(name)
+    tiles = jnp.stack([x for _ in range(peers)])
+    tiles = lax.all_to_all(tiles, name, split_axis=0, concat_axis=0)
+    return jnp.concatenate(tiles, axis=along)
 
 
 def partner(shard, axis, apart):
@@ -34,7 +41,7 @@
         * value_scale
     ).astype(jnp.bfloat16)
     all_keys, all_values = (
-        lax.all_gather(key_states[0], "ctx", axis=0, tiled=True),
+        all_by_exchange(key_states[0], "ctx", 0),
         lax.all_gather(local_values, "ctx", axis=0, tiled=True),
     )
     seq_total = all_keys.shape[0]

time: 347 us -> 334 us (0.963)
  waiting for transfers between devices: 216 us -> 190 us
  starting transfers between devices: 16.4 us -> 22.8 us
  local copies, waits for them, and re-layouts: 15.5 us -> 21.1 us
    all_to_all x0 -> x1, waiting for transfers between devices: none -> 33.3 us  [all_by_exchange(): tiles = lax.all_to_all(tiles, name, split_axis=0, concat_axis=0)]
    all_gather x1 -> x0, waiting for transfers between devices: 27.6 us -> none  [local(): lax.all_gather(key_states[0], 'ctx', axis=0, tiled=True)]
    all_gather x1, waiting for transfers between devices: 64.3 us -> 44.6 us  [local(): lax.all_gather(own_weight, 'ctx', axis=0, tiled=True)]
    all_gather x1, waiting for transfers between devices: 31 us -> 19.1 us  [local(): lax.all_gather(local_values, 'ctx', axis=0, tiled=True)]
    all_to_all x0 -> x1, starting transfers between devices: none -> 10.3 us  [all_by_exchange(): tiles = lax.all_to_all(tiles, name, split_axis=0, concat_axis=0)]
    all_to_all x1, starting transfers between devices: 10.3 us -> 6.5 us  [local(): lax.all_to_all(token_block, 'ctx', split_axis=1, concat_axis=0, tiled=True)]
    another operation x0 -> x3, local copies, waits for them, and re-layouts: none -> 3.65 us  [the longest x1 1.51 us: local(): key_heads = all_keys.reshape(seq_total, KV_HEADS, HEAD_DIM)]
    unnamed x13 -> x8, local copies, waits for them, and re-layouts: 9.48 us -> 7.77 us
  transfers between devices with their start and end apart: 5 -> 5, of which waited for: 4 -> 4; matrix products, arithmetic and copies ran while one was open for 6% -> 8% of each run, Pallas kernels for 0% -> 0%
where the time goes in v1:
time: 334 us; the launch traced here: 333 us
  waiting for transfers between devices  190 us (57%)
  blocking collectives  62.7 us (19%)
  starting transfers between devices  22.8 us (7%)
  matrix products  21.8 us (7%)
  local copies, waits for them, and re-layouts  21.1 us (6%)
  between operations  14.1 us (4%)
    ppermute x1, waiting for transfers between devices, partner(): lax.ppermute(shard, axis, [(i, i ^ 1 << apart) for i in range(lax.axis_si...  92.1 us
    psum x1, blocking collectives, local(): value_cot16 = lax.psum(value_terms, 'ctx').astype(jnp.bfloat16)  62.7 us
    all_gather x1, waiting for transfers between devices, local(): lax.all_gather(own_weight, 'ctx', axis=0, tiled=True)  44.6 us
    all_to_all x1, waiting for transfers between devices, all_by_exchange(): tiles = lax.all_to_all(tiles, name, split_axis=0, concat_axis=0)  33.3 us
    all_gather x1, waiting for transfers between devices, local(): lax.all_gather(local_values, 'ctx', axis=0, tiled=True)  19.1 us
    all_to_all x1, starting transfers between devices, all_by_exchange(): tiles = lax.all_to_all(tiles, name, split_axis=0, concat_axis=0)  10.3 us
    dot_general x1, matrix products, local(): jnp.einsum('kgij,ikgd->jkd', probabilities, cot_heads, preferred_element_...  8.46 us
    unnamed x8, local copies, waits for them, and re-layouts  7.77 us
  transfers between devices with their start and end apart: 5, of which 4 were waited for; matrix products, arithmetic and copies ran while one was open for 8% of the time, Pallas kernels for 0%

profile of v1, /device:TPU:1, one launch (start us, length us, event | category | flops | bytes accessed | tf_op | source)
XLA Modules:
  0.0 333.2 jit_solution(6353384324297421988)
XLA Ops:
  7.2 0.0 copy-start
  7.2 0.0 all-gather.6.cloned.1.call-start
  7.2 0.7 all-gather.6.cloned.1.call-update
  7.9 1.0 copy.43
  8.9 1.1 stack.12
  10.1 10.3 %all-to-all-start = ((bf16[8,128,512]{1,2,0:T(8,128)(2,1)}), bf16[8,128,512]{1,2,0:T(8,128)(2,1)S(1)}, u32[]{:S(2)}, u32[]{:S(2)}) async-start(bf16[8,128,512]{1,2,0:T(8,128)(2,1)} %stack.12), calls=%async_computation | async-start | bytes 2097152 | tf_op jit(solution)/shard_map/all_to_all | solution.py:17
  20.4 2.2 copy.51
  22.6 33.3 %all-to-all-done = bf16[8,128,512]{1,2,0:T(8,128)(2,1)S(1)} async-done(((bf16[8,128,512]{1,2,0:T(8,128)(2,1)}), bf16[8,128,512]{1,2,0:T(8,128)(2,1)S(1)}, u32[]{:S(2)}, u32[]{:S(2)}) %all-to-all-start) | async-done | bytes 1048608 | tf_op jit(solution)/shard_map/all_to_all | solution.py:17
  55.9 6.5 %all-to-all-start.1 = ((bf16[128,8,512]{0,2,1:T(8,128)(2,1)}), bf16[128,8,512]{0,2,1:T(8,128)(2,1)S(1)}, u32[]{:S(2)}, u32[]{:S(2)}) async-start(bf16[128,8,512]{0,2,1:T(8,128)(2,1)} %bitcast.16), calls=%async_computation.1 | async-start | bytes 2097152 | tf_op jit(solution)/shard_map/all_to_all | solution.py:34
  62.4 0.0 all-gather.4.cloned.1.call-start
  62.4 44.6 %all-gather.6.cloned.1.call-done = bf16[1,4096,512]{2,1,0:T(8,128)(2,1)} async-done(((bf16[1,512,512]{2,1,0:T(8,128)(2,1)}), bf16[1,4096,512]{2,1,0:T(8,128)(2,1)}) %all-gather.6.cloned.1.call-update) | async-done | bytes 4194320 | tf_op jit(solution)/shard_map/all_gather | solution.py:38
  106.9 3.9 %fusion.19 = bf16[128,512]{1,0:T(8,128)(2,1)} fusion(bf16[1,4096,512]{2,1,0:T(8,128)(2,1)} %all-gather.6.cloned.1.call-done, bf16[1,128,4096]{2,1,0:T(8,128)(2,1)} %param.7), kind=kOutput, calls=%fused_computation.22 | convolution fusion | flops 537001984 | bytes 5373952 | tf_op jit(solution)/shard_map/dot_general | solution.py:36
  110.8 0.0 all-gather.4.cloned.1.call-update
  110.9 0.0 copy-done
  110.9 0.2 copy.41
  111.1 2.2 reshape_squeeze.3
  113.3 2.2 copy.49
  115.5 1.3 copy.42
  116.8 2.0 copy.53
  118.8 0.1 iota_compare_fusion
  118.9 1.7 copy.44
  120.6 1.5 reshape_reshape.3
  122.1 0.0 all-to-all-done.1
  122.1 1.3 copy.52
  123.4 7.0 %fusion.48 = (f32[4,4,128]{2,1,0:T(4,128)S(1)}, f32[4,4,128,1024]{2,3,1,0:T(8,128)}) fusion(pred[128,1024]{0,1:T(8,128)(4,1)S(1)} %iota_compare_fusion, bf16[1024,4,128]{0,2,1:T(8,128)(2,1)S(1)} %reshape_reshape.3, bf16[128,4,4,128]{3,2,1,0:T(4,128)(2,1)} %reshape_squeeze.3), kind=kOutput, calls=%fused_computation.48 | convolution fusion | flops 545260544 | bytes 10100736 | tf_op jit(solution)/shard_map/sub | solution.py:59
  130.4 19.1 %all-gather.4.cloned.1.call-done = bf16[1024,512]{1,0:T(8,128)(2,1)} async-done(((bf16[128,512]{1,0:T(8,128)(2,1)}), bf16[1024,512]{1,0:T(8,128)(2,1)}) %all-gather.4.cloned.1.call-update) | async-done | bytes 1048592 | tf_op jit(solution)/shard_map/all_gather | solution.py:45
  149.5 2.3 copy.61
  151.7 8.5 %fusion.15 = f32[4,128,1024,1]{2,1,3,0:T(8,128)S(1)} fusion(f32[128,4,4,128]{0,3,2,1:T(8,128)} %bitcast.113, bf16[1024,4,128,1]{0,2,3,1:T(8,128)(2,1)} %bitcast.115, f32[4,4,128,1024]{2,3,1,0:T(8,128)} %get-tuple-element.13, f32[4,4,128]{2,1,0:T(4,128)S(1)} %get-tuple-element.12), kind=kOutput, calls=%fused_computation.20 | convolution fusion | flops 1082916864 | bytes 12591104 | tf_op jit(solution)/shard_map/kgij,ikgd->jkd/dot_general | solution.py:67
  160.2 62.7 %all-reduce.1 = bf16[1024,512]{0,1:T(8,128)(2,1)} all-reduce(f32[1024,512]{0,1:T(8,128)S(1)} %bitcast.112), channel_id=1, replica_groups=mesh['rep'=64,'ctx'=8] {'ctx'}, use_global_device_ids=true, to_apply=%region_2.3 | all-reduce | flops 524288 | bytes 3145728 | tf_op jit(solution)/shard_map/psum | solution.py:71
  222.9 2.5 fusion.13
  225.4 0.2 fusion.37
  225.6 0.2 pad_maximum_fusion
  225.8 6.0 %collective-permute-start = (f32[2,512,512]{1,2,0:T(8,128)S(1)}, f32[2,512,512]{1,2,0:T(8,128)S(1)}, u32[]{:S(2)}, u32[]{:S(2)}) collective-permute-start(f32[2,512,512]{1,2,0:T(8,128)S(1)} %pad_maximum_fusion), channel_id=1, source_target_pairs={{0,64},{8,72},{16,80},{24,88},{32,96},{40,104},{48,112},{56,120},{... | collective-permute-start | bytes 6291464 | tf_op jit(solution)/shard_map/ppermute | solution.py:22
  231.8 92.1 %collective-permute-done = f32[2,512,512]{1,2,0:T(8,128)S(1)} collective-permute-done((f32[2,512,512]{1,2,0:T(8,128)S(1)}, f32[2,512,512]{1,2,0:T(8,128)S(1)}, u32[]{:S(2)}, u32[]{:S(2)}) %collective-permute-start) | collective-permute-done | bytes 2097184 | tf_op jit(solution)/shard_map/ppermute | solution.py:22
  323.9 0.5 fusion.39
  324.4 1.0 copy.54
  325.4 1.0 copy.55
  (1 shorter events, 0.0 us)
Async XLA Ops:
  7.2 103.7 %copy-start = (bf16[1,512,512]{2,1,0:T(8,128)(2,1)S(1)}, bf16[1,512,512]{2,1,0:T(8,128)(2,1)}, u32[]{:S(2)}) copy-start(bf16[1,512,512]{2,1,0:T(8,128)(2,1)} %param.11) | copy-start | bytes 1572868
  7.2 99.8 %all-gather.6.cloned.1.call-start = ((), (), s32[]{:S(2)}) async-start(), calls=%async_computation.3 | async-start | bytes 4718592 | tf_op jit(solution)/shard_map/all_gather | solution.py:38
  10.1 45.8 %all-to-all-start = ((bf16[8,128,512]{1,2,0:T(8,128)(2,1)}), bf16[8,128,512]{1,2,0:T(8,128)(2,1)S(1)}, u32[]{:S(2)}, u32[]{:S(2)}) async-start(bf16[8,128,512]{1,2,0:T(8,128)(2,1)} %stack.12), calls=%async_computation | async-start | bytes 2097152 | tf_op jit(solution)/shard_map/all_to_all | solution.py:17
  55.9 66.2 %all-to-all-start.1 = ((bf16[128,8,512]{0,2,1:T(8,128)(2,1)}), bf16[128,8,512]{0,2,1:T(8,128)(2,1)S(1)}, u32[]{:S(2)}, u32[]{:S(2)}) async-start(bf16[128,8,512]{0,2,1:T(8,128)(2,1)} %bitcast.16), calls=%async_computation.1 | async-start | bytes 2097152 | tf_op jit(solution)/shard_map/all_to_all | solution.py:34
  62.4 87.1 %all-gather.4.cloned.1.call-start = ((), (), s32[]{:S(2)}) async-start(), calls=%async_computation.2 | async-start | bytes 1179648 | tf_op jit(solution)/shard_map/all_gather | solution.py:45
  225.8 98.1 %collective-permute-start = (f32[2,512,512]{1,2,0:T(8,128)S(1)}, f32[2,512,512]{1,2,0:T(8,128)S(1)}, u32[]{:S(2)}, u32[]{:S(2)}) collective-permute-start(f32[2,512,512]{1,2,0:T(8,128)S(1)} %pad_maximum_fusion), channel_id=1, source_target_pairs={{0,64},{8,72},{16,80},{24,88},{32,96},{40,104},{48,112},{56,120},{... | collective-permute-start | bytes 6291464 | tf_op jit(solution)/shard_map/ppermute | solution.py:22
Sparse Core Ops, SparseCore 0:
  10.1 96.8 all-gather.5
  111.0 38.4 all-gather.3
